TPU v7x, 32 devices: a whole 2x2x4 slice. The times are simulated.
32 devices in a mesh: groups: 2 (over y), chan: 8 (over z, x), pair: 2 (over core).
Axes of the slice: x: 2, y: 2, z: 4, core: 2. Of those that a mesh axis runs over, the one named last changes fastest.
Arguments:
- raw: bfloat16 [1024, 1, 12000], P(('groups', 'chan')), parts along dimension 0, may hold values from -6 to 6
- live_index: int32 [16, 64], P(('groups', 'chan')), parts along dimension 0, may hold values from 0 to 63, each once within a row
- live_count: int32 [16], P('groups'), parts along dimension 0, may hold values from 1 to 64, 256 in all
Outputs:
- correlation: bfloat16 [6, 1024, 512], P('pair', ('groups', 'chan')), parts along dimension 1
There are 2 independent parts, one for each index of `groups`. A program takes and returns all parts, laid end to end along the dimension named above; each array names one. Nothing has to cross between parts.
Inputs may be any that keep to these rules, and one draw needn't show every extreme that they name: `live_index`: each block's row is a permutation of the raw channels of that block. `live_count`: live slots of each block; they sum to 256, and some block fills all 64 slots.
All inputs are finite; a program needn't handle non-finite values.
Results may differ from a plain program's by a relative error of at most 0.001.
The roundings to bfloat16 on the way count: a program that leaves them out, or rounds other values in their place, can miss the bound.
Values may be sent and summed in bfloat16 or wider, within the bound.
A program may use at most 128 MiB of HBM per device.

v0:
```python
import jax
import jax.numpy as jnp
from jax import lax
from jax.sharding import PartitionSpec as P

S = 12000
NB = 448
NSEG = 1
L = 6
LSTEP = 125
F0 = 60


water_level = 0.1


def lag_weights(lag_ids, bin_ids):
    band_taper = 0.5 - 0.5 * jnp.cos(2.0 * jnp.pi * (bin_ids.astype(jnp.float32) + 0.5) / NB)
    phase_int = (F0 + bin_ids)[None, :] * lag_ids[:, None] % S
    waves = jnp.cos(phase_int.astype(jnp.float32) * (2.0 * jnp.pi / S))
    return band_taper[None, :] * waves / jnp.sqrt(jnp.float32(NSEG * NB))


def spectra_of(picked_rows, bins, samples):
    block_len = samples // 8

    def add_block(block_id, running):
        sample_ids = block_id * block_len + jnp.arange(block_len, dtype=jnp.int32)
        phase_int = sample_ids[:, None] * (F0 + bins)[None, :] % samples
        angles = phase_int.astype(jnp.float32) * (2.0 * jnp.pi / samples)
        dft_table = jnp.concatenate([jnp.cos(angles), -jnp.sin(angles)], axis=1).astype(
            jnp.bfloat16
        )
        sample_blk = lax.dynamic_slice_in_dim(picked_rows, block_id * block_len, block_len, 1)
        return running + jnp.dot(sample_blk, dft_table, preferred_element_type=jnp.float32)

    start_acc = jnp.zeros((picked_rows.shape[0], 2 * bins.shape[0]), jnp.float32)
    return lax.fori_loop(0, 8, add_block, start_acc)


def whiten(spectrum, band_power):
    magnitude = spectrum[:, :, 0] ** 2 + spectrum[:, :, 1] ** 2
    denom = jnp.sqrt(magnitude + water_level * band_power[:, :, None] + 1e-06)
    return (spectrum / denom[:, :, None, :]).astype(jnp.bfloat16)


def correlate(lag_rows, columns):
    product = lax.dot_general(
        lag_rows, columns, (((1,), (1,)), ((), ())), preferred_element_type=jnp.float32
    )
    return product.astype(jnp.bfloat16)


def shards(raw, live_index, live_count):
    slot_count = raw.shape[0]
    seg_count = raw.shape[1]
    samples = raw.shape[2]
    pair_count = lax.axis_size("pair")
    pair_index = lax.axis_index("pair")
    chan_index = lax.axis_index("chan")
    local_bins = NB // pair_count
    lag_share = L // pair_count
    live_slots = live_count[chan_index]
    slot_ids = jnp.arange(slot_count, dtype=jnp.int32)
    chosen = jnp.take(raw, live_index[0], axis=0)
    picked = jnp.where((slot_ids < live_slots)[:, None, None], chosen, jnp.zeros((), raw.dtype))
    picked_rows = picked.reshape(slot_count * seg_count, samples)
    own_bins = pair_index * local_bins + jnp.arange(local_bins, dtype=jnp.int32)
    spectrum = spectra_of(picked_rows, own_bins, samples).reshape(
        slot_count, seg_count, 2, local_bins
    )
    band_power = lax.psum(jnp.sum(spectrum * spectrum, axis=(2, 3)), "pair") / NB
    own_half = whiten(spectrum, band_power)
    own_full = lax.all_gather(own_half, "pair", axis=3, tiled=True)
    own_lags = (pair_index * lag_share + jnp.arange(lag_share, dtype=jnp.int32)) * LSTEP
    weights = lag_weights(own_lags, jnp.arange(NB, dtype=jnp.int32))
    lag_rows = (own_full[None] * weights[:, None, None, None, :]).astype(jnp.bfloat16)
    lag_rows = lag_rows.reshape(lag_share * slot_count, -1)
    own_rows = own_full.reshape(slot_count, -1)
    product = correlate(lag_rows, lax.all_gather(own_rows, "chan", axis=0, tiled=True))
    correlation = product.reshape(lag_share, slot_count, -1)
    return correlation


def solution(mesh):
    return jax.shard_map(
        shards,
        mesh=mesh,
        in_specs=(P(("groups", "chan"), None, None), P(("groups", "chan"), None), P("groups")),
        out_specs=P("pair", ("groups", "chan"), None),
        check_vma=False,
    )
```

profile of v0, /device:TPU:0, one launch (start us, length us, event | category | flops | bytes accessed | tf_op | source)
XLA Modules:
  0.0 118.7 jit_solution(9967840530059940738)
XLA Ops:
  0.0 1.4 %dynamic_slice.13 = s32[1]{0:T(128)} dynamic-slice(s32[8]{0:T(128)} %param.7, s32[]{:T(128)S(6)} %select_n.73), dynamic_slice_sizes={1} | dynamic-slice | bytes 12 | tf_op jit(solution)/shard_map/dynamic_slice | solution.py:63
  1.4 1.3 %compare_and_fusion = (pred[64]{0:T(512)(128)(4,1)S(1)}, pred[64]{0:T(512)(128)(4,1)S(1)}) fusion(s32[1,64]{1,0:T(1,128)} %param.6, s32[]{:T(128)} %bitcast), kind=kLoop, calls=%fused_computation.49 | loop fusion | flops 448 | bytes 388 | tf_op jit(solution)/shard_map/jit(_take)/and | solution.py:65
  3.3 1.5 %gather_fusion = bf16[64,12000]{1,0:T(8,128)(2,1)S(1)} fusion(bf16[64,12000]{1,0:T(8,128)(2,1)S(1)} %bitcast.21, s32[1024]{0:T(1024)S(1)} %pad_clamp_fusion), kind=kCustom, calls=%fused_computation | custom fusion | bytes 3072256 | tf_op jit(solution)/shard_map/jit(_take)/gather | solution.py:65
  4.9 1.4 %select_select_fusion = bf16[64,12000]{1,0:T(8,128)(2,1)} fusion(bf16[64,12000]{1,0:T(8,128)(2,1)S(1)} %gather_fusion, pred[64]{0:T(512)(128)(4,1)S(1)} %get-tuple-element.147, pred[64]{0:T(512)(128)(4,1)S(1)} %get-tuple-element.148), kind=kLoop, calls=%fused_computation.21 | loop fusion | flops 1536000 | bytes 3072128 | tf_op jit(solution)/shard_map/jit(_where)/select_n | solution.py:66
  6.3 70.3 %while.16 = (s32[]{:T(128)}, f32[64,448]{1,0:T(8,128)S(1)}, bf16[64,12000]{1,0:T(8,128)(2,1)}, s32[]{:T(128)}, s32[]{:T(128)}, /*index=5*/s32[]{:T(128)}, s32[]{:T(128)}, s32[]{:T(128)}) while((s32[]{:T(128)}, f32[64,448]{1,0:T(8,128)S(1)}, bf16[64,12000]{1,0:T(8,128)(2,1)}, s32[]{:T(128)}, s32[]{:T(128)}, /*index=5*/s32[]{:T(128)}, ...), condition=%wide.region_1.2_spmd.clone, body=%wide.region_0.1_spmd.clone.sunk | while | flops 92795296 | bytes 3127929 | solution.py:38
  6.3 7.1 %cosine_convert_fusion.2 = (bf16[1500,224]{1,0:T(8,128)(2,1)S(1)}, bf16[1500,224]{1,0:T(8,128)(2,1)S(1)}) fusion(s32[224]{0:T(256)S(1)} %add_add_fusion.2, s32[1500]{0:T(1024)S(1)} %iota_add_fusion.3), kind=kLoop, calls=%fused_computation.10.clone.1 | loop fusion | flops 4032000 | bytes 1350896 | tf_op jit(solution)/shard_map/convert
  13.4 1.6 %fusion.39 = f32[64,448]{1,0:T(8,128)S(1)} fusion(bf16[1500,224]{1,0:T(8,128)(2,1)S(1)} %get-tuple-element.176, bf16[1500,224]{1,0:T(8,128)(2,1)S(1)} %get-tuple-element.177, bf16[64,12000]{1,0:T(8,128)(2,1)} %get-tuple-element.196, s32[]{:T(128)S(6)} %select_n.112, f32[64,448]{1,0:T(8,128)S(1)} %get-tuple-element.187, pred[]{:T(512)S(6)} %compare.3), kind=kOutput, calls=%fused_computation.15.clone.1 | convolution fusion | flops 88761344 | bytes 1769989 | tf_op jit(solution)/shard_map/while/body/eval_jaxpr/dot_general | solution.py:35
  15.1 7.1 %cosine_convert_fusion.2 = (bf16[1500,224]{1,0:T(8,128)(2,1)S(1)}, bf16[1500,224]{1,0:T(8,128)(2,1)S(1)}) fusion(s32[224]{0:T(256)S(1)} %add_add_fusion.2, s32[1500]{0:T(1024)S(1)} %iota_add_fusion.3), kind=kLoop, calls=%fused_computation.10.clone.1 | loop fusion | flops 4032000 | bytes 1350896 | tf_op jit(solution)/shard_map/convert
  22.2 1.6 %fusion.39 = f32[64,448]{1,0:T(8,128)S(1)} fusion(bf16[1500,224]{1,0:T(8,128)(2,1)S(1)} %get-tuple-element.176, bf16[1500,224]{1,0:T(8,128)(2,1)S(1)} %get-tuple-element.177, bf16[64,12000]{1,0:T(8,128)(2,1)} %get-tuple-element.196, s32[]{:T(128)S(6)} %select_n.112, f32[64,448]{1,0:T(8,128)S(1)} %get-tuple-element.187, pred[]{:T(512)S(6)} %compare.3), kind=kOutput, calls=%fused_computation.15.clone.1 | convolution fusion | flops 88761344 | bytes 1769989 | tf_op jit(solution)/shard_map/while/body/eval_jaxpr/dot_general | solution.py:35
  23.9 7.1 %cosine_convert_fusion.2 = (bf16[1500,224]{1,0:T(8,128)(2,1)S(1)}, bf16[1500,224]{1,0:T(8,128)(2,1)S(1)}) fusion(s32[224]{0:T(256)S(1)} %add_add_fusion.2, s32[1500]{0:T(1024)S(1)} %iota_add_fusion.3), kind=kLoop, calls=%fused_computation.10.clone.1 | loop fusion | flops 4032000 | bytes 1350896 | tf_op jit(solution)/shard_map/convert
  31.0 1.6 %fusion.39 = f32[64,448]{1,0:T(8,128)S(1)} fusion(bf16[1500,224]{1,0:T(8,128)(2,1)S(1)} %get-tuple-element.176, bf16[1500,224]{1,0:T(8,128)(2,1)S(1)} %get-tuple-element.177, bf16[64,12000]{1,0:T(8,128)(2,1)} %get-tuple-element.196, s32[]{:T(128)S(6)} %select_n.112, f32[64,448]{1,0:T(8,128)S(1)} %get-tuple-element.187, pred[]{:T(512)S(6)} %compare.3), kind=kOutput, calls=%fused_computation.15.clone.1 | convolution fusion | flops 88761344 | bytes 1769989 | tf_op jit(solution)/shard_map/while/body/eval_jaxpr/dot_general | solution.py:35
  32.6 7.1 %cosine_convert_fusion.2 = (bf16[1500,224]{1,0:T(8,128)(2,1)S(1)}, bf16[1500,224]{1,0:T(8,128)(2,1)S(1)}) fusion(s32[224]{0:T(256)S(1)} %add_add_fusion.2, s32[1500]{0:T(1024)S(1)} %iota_add_fusion.3), kind=kLoop, calls=%fused_computation.10.clone.1 | loop fusion | flops 4032000 | bytes 1350896 | tf_op jit(solution)/shard_map/convert
  39.8 1.6 %fusion.39 = f32[64,448]{1,0:T(8,128)S(1)} fusion(bf16[1500,224]{1,0:T(8,128)(2,1)S(1)} %get-tuple-element.176, bf16[1500,224]{1,0:T(8,128)(2,1)S(1)} %get-tuple-element.177, bf16[64,12000]{1,0:T(8,128)(2,1)} %get-tuple-element.196, s32[]{:T(128)S(6)} %select_n.112, f32[64,448]{1,0:T(8,128)S(1)} %get-tuple-element.187, pred[]{:T(512)S(6)} %compare.3), kind=kOutput, calls=%fused_computation.15.clone.1 | convolution fusion | flops 88761344 | bytes 1769989 | tf_op jit(solution)/shard_map/while/body/eval_jaxpr/dot_general | solution.py:35
  41.4 7.1 %cosine_convert_fusion.2 = (bf16[1500,224]{1,0:T(8,128)(2,1)S(1)}, bf16[1500,224]{1,0:T(8,128)(2,1)S(1)}) fusion(s32[224]{0:T(256)S(1)} %add_add_fusion.2, s32[1500]{0:T(1024)S(1)} %iota_add_fusion.3), kind=kLoop, calls=%fused_computation.10.clone.1 | loop fusion | flops 4032000 | bytes 1350896 | tf_op jit(solution)/shard_map/convert
  48.5 1.6 %fusion.39 = f32[64,448]{1,0:T(8,128)S(1)} fusion(bf16[1500,224]{1,0:T(8,128)(2,1)S(1)} %get-tuple-element.176, bf16[1500,224]{1,0:T(8,128)(2,1)S(1)} %get-tuple-element.177, bf16[64,12000]{1,0:T(8,128)(2,1)} %get-tuple-element.196, s32[]{:T(128)S(6)} %select_n.112, f32[64,448]{1,0:T(8,128)S(1)} %get-tuple-element.187, pred[]{:T(512)S(6)} %compare.3), kind=kOutput, calls=%fused_computation.15.clone.1 | convolution fusion | flops 88761344 | bytes 1769989 | tf_op jit(solution)/shard_map/while/body/eval_jaxpr/dot_general | solution.py:35
  50.2 7.1 %cosine_convert_fusion.2 = (bf16[1500,224]{1,0:T(8,128)(2,1)S(1)}, bf16[1500,224]{1,0:T(8,128)(2,1)S(1)}) fusion(s32[224]{0:T(256)S(1)} %add_add_fusion.2, s32[1500]{0:T(1024)S(1)} %iota_add_fusion.3), kind=kLoop, calls=%fused_computation.10.clone.1 | loop fusion | flops 4032000 | bytes 1350896 | tf_op jit(solution)/shard_map/convert
  57.3 1.6 %fusion.39 = f32[64,448]{1,0:T(8,128)S(1)} fusion(bf16[1500,224]{1,0:T(8,128)(2,1)S(1)} %get-tuple-element.176, bf16[1500,224]{1,0:T(8,128)(2,1)S(1)} %get-tuple-element.177, bf16[64,12000]{1,0:T(8,128)(2,1)} %get-tuple-element.196, s32[]{:T(128)S(6)} %select_n.112, f32[64,448]{1,0:T(8,128)S(1)} %get-tuple-element.187, pred[]{:T(512)S(6)} %compare.3), kind=kOutput, calls=%fused_computation.15.clone.1 | convolution fusion | flops 88761344 | bytes 1769989 | tf_op jit(solution)/shard_map/while/body/eval_jaxpr/dot_general | solution.py:35
  59.0 7.1 %cosine_convert_fusion.2 = (bf16[1500,224]{1,0:T(8,128)(2,1)S(1)}, bf16[1500,224]{1,0:T(8,128)(2,1)S(1)}) fusion(s32[224]{0:T(256)S(1)} %add_add_fusion.2, s32[1500]{0:T(1024)S(1)} %iota_add_fusion.3), kind=kLoop, calls=%fused_computation.10.clone.1 | loop fusion | flops 4032000 | bytes 1350896 | tf_op jit(solution)/shard_map/convert
  66.1 1.6 %fusion.39 = f32[64,448]{1,0:T(8,128)S(1)} fusion(bf16[1500,224]{1,0:T(8,128)(2,1)S(1)} %get-tuple-element.176, bf16[1500,224]{1,0:T(8,128)(2,1)S(1)} %get-tuple-element.177, bf16[64,12000]{1,0:T(8,128)(2,1)} %get-tuple-element.196, s32[]{:T(128)S(6)} %select_n.112, f32[64,448]{1,0:T(8,128)S(1)} %get-tuple-element.187, pred[]{:T(512)S(6)} %compare.3), kind=kOutput, calls=%fused_computation.15.clone.1 | convolution fusion | flops 88761344 | bytes 1769989 | tf_op jit(solution)/shard_map/while/body/eval_jaxpr/dot_general | solution.py:35
  67.8 7.1 %cosine_convert_fusion.2 = (bf16[1500,224]{1,0:T(8,128)(2,1)S(1)}, bf16[1500,224]{1,0:T(8,128)(2,1)S(1)}) fusion(s32[224]{0:T(256)S(1)} %add_add_fusion.2, s32[1500]{0:T(1024)S(1)} %iota_add_fusion.3), kind=kLoop, calls=%fused_computation.10.clone.1 | loop fusion | flops 4032000 | bytes 1350896 | tf_op jit(solution)/shard_map/convert
  74.9 1.6 %fusion.39 = f32[64,448]{1,0:T(8,128)S(1)} fusion(bf16[1500,224]{1,0:T(8,128)(2,1)S(1)} %get-tuple-element.176, bf16[1500,224]{1,0:T(8,128)(2,1)S(1)} %get-tuple-element.177, bf16[64,12000]{1,0:T(8,128)(2,1)} %get-tuple-element.196, s32[]{:T(128)S(6)} %select_n.112, f32[64,448]{1,0:T(8,128)S(1)} %get-tuple-element.187, pred[]{:T(512)S(6)} %compare.3), kind=kOutput, calls=%fused_computation.15.clone.1 | convolution fusion | flops 88761344 | bytes 1769989 | tf_op jit(solution)/shard_map/while/body/eval_jaxpr/dot_general | solution.py:35
  76.9 2.6 %psum.7 = f32[64,1]{0,1:T(1,128)S(1)} all-reduce(f32[64,1]{0,1:T(1,128)S(1)} %bitcast.22), channel_id=1, replica_groups=mesh['groups'=2,'chan'=8,'pair'=2] {'pair'}, use_global_device_ids=true, to_apply=%region_3.4 | all-reduce | flops 64 | bytes 512 | tf_op jit(solution)/shard_map/psum | solution.py:72
  79.9 2.0 %all_gather.6 = bf16[64,1,2,448]{0,2,1,3:T(2,128)(2,1)S(1)} all-gather(bf16[64,1,2,224]{0,2,1,3:T(2,128)(2,1)S(1)} %copy.10), channel_id=1, replica_groups=mesh['groups'=2,'chan'=8,'pair'=2] {'pair'}, dimensions={3}, use_global_device_ids=true | all-gather | bytes 172032 | tf_op jit(solution)/shard_map/all_gather | solution.py:74
  83.4 34.2 %all_gather.7 = bf16[512,896]{1,0:T(8,128)(2,1)S(1)} all-gather(bf16[64,896]{1,0:T(8,128)(2,1)S(1)} %reshape.206), channel_id=1, replica_groups=mesh['groups'=2,'chan'=8,'pair'=2] {'chan'}, dimensions={0}, use_global_device_ids=true | all-gather | bytes 1032192 | tf_op jit(solution)/shard_map/all_gather | solution.py:80
  (39 shorter events, 4.0 us)
Async XLA Ops:
  0.0 3.3 %copy-start = (bf16[64,1,12000]{2,0,1:T(8,128)(2,1)S(1)}, bf16[64,1,12000]{2,0,1:T(8,128)(2,1)}, u32[]{:S(2)}) copy-start(bf16[64,1,12000]{2,0,1:T(8,128)(2,1)} %param.5) | copy-start | bytes 4608004
where the time goes:
time: 119 us
  other arithmetic  61.1 us (51%)
  blocking collectives  38.8 us (33%)
  matrix products  14.2 us (12%)
  local copies, waits for them, and re-layouts  4.09 us (3%)
    another operation x8, other arithmetic  56.7 us
    all_gather x1, blocking collectives, shards(): lax.all_gather(own_rows, 'chan', axis=0, tiled=True)  34.2 us
    dot_general x8, matrix products, add_block(): jnp.dot(sample_blk, dft_table, preferred_element_type=jnp.float32)  13.1 us
    psum x1, blocking collectives, shards(): lax.psum(jnp.sum(spectrum * spectrum, axis=(2, 3)), 'pair') / NB  2.63 us

commit v1 on v0

v1 whole, which is shorter than its diff:
```python
import functools

import jax
import jax.numpy as jnp
import numpy as np
from jax import lax
from jax.experimental import pallas as pl
from jax.experimental.pallas import tpu as pltpu
from jax.sharding import PartitionSpec as P

S = 12000
NB = 448
L = 6
LSTEP = 125
F0 = 60
WATER = 0.1
QUARTER = S // 4
CHUNK = 256
NCHUNK = -(-QUARTER // CHUNK)
PADB = 512
COLS = 2 * NB


def phase_rows(steps):
    k = F0 + np.arange(NB)
    angle = 2.0 * np.pi * ((np.asarray(steps)[:, None] * k[None, :]) % S) / S
    out = np.zeros((len(steps), 2 * PADB), np.float32)
    out[:, :NB] = np.cos(angle)
    out[:, PADB : PADB + NB] = -np.sin(angle)
    return out


def twiddles():
    fine = phase_rows(np.arange(16))
    mid = phase_rows(16 * np.arange(16))
    return np.concatenate([fine, mid], axis=0)


def coarse_twiddles():
    coarse = phase_rows(CHUNK * np.arange(NCHUNK))
    return np.repeat(coarse[:, None, :], 8, axis=1)


def column_bins():
    tail = np.arange(384, NB)
    return np.concatenate([np.arange(384), np.arange(384), tail, tail])


def lag_table():
    j = column_bins()
    taper = 0.5 - 0.5 * np.cos(2.0 * np.pi * (j + 0.5) / NB)
    lags = np.arange(L)[:, None] * LSTEP
    waves = np.cos(2.0 * np.pi * (((F0 + j)[None, :] * lags) % S) / S)
    table = np.zeros((2, 8, COLS), np.float32)
    table[:, : L // 2] = (taper[None, :] * waves / np.sqrt(NB)).reshape(2, L // 2, COLS)
    return table


def make_table(tw_ref, coarse_ref, base_ref, table_ref):
    for a in range(16):
        for v in range(PADB // 128):
            c_cols = slice(128 * v, 128 * v + 128)
            s_cols = slice(PADB + 128 * v, PADB + 128 * v + 128)
            fc, fs = tw_ref[0:16, c_cols], tw_ref[0:16, s_cols]
            mc, ms = tw_ref[16 + a : 17 + a, c_cols], tw_ref[16 + a : 17 + a, s_cols]
            base_ref[16 * a : 16 * a + 16, c_cols] = fc * mc - fs * ms
            base_ref[16 * a : 16 * a + 16, s_cols] = fs * mc + fc * ms

    def chunk(i, carry):
        row0 = pl.multiple_of(i * CHUNK, CHUNK)
        for v in range(PADB // 128):
            c_cols = slice(128 * v, 128 * v + 128)
            s_cols = slice(PADB + 128 * v, PADB + 128 * v + 128)
            cc = coarse_ref[i, 0:1, c_cols]
            cs = coarse_ref[i, 0:1, s_cols]
            for r in range(0, CHUNK, 16):
                bc, bs = base_ref[r : r + 16, c_cols], base_ref[r : r + 16, s_cols]
                rows = pl.ds(row0 + r, 16)
                table_ref[rows, c_cols] = (bc * cc - bs * cs).astype(jnp.bfloat16)
                table_ref[rows, s_cols] = (bs * cc + bc * cs).astype(jnp.bfloat16)
        return carry

    lax.fori_loop(0, NCHUNK, chunk, 0)


def whiten_rows(spec_ref, slots):
    def quarter(q, part):
        return spec_ref[slots * q : slots * (q + 1), PADB * part : PADB * (part + 1)]

    a0, a1, a2, a3 = (quarter(q, 0) for q in range(4))
    b0, b1, b2, b3 = (quarter(q, 1) for q in range(4))
    m = lax.broadcasted_iota(jnp.int32, (slots, PADB), 1) % 4
    even = m % 2 == 0
    sign = jnp.where(m < 2, 1.0, -1.0)
    re = jnp.where(even, a0 + a2 + sign * (a1 + a3), a0 - a2 + sign * (b1 - b3))
    im = jnp.where(even, b0 + b2 + sign * (b1 + b3), b0 - b2 - sign * (a1 - a3))
    mag = re * re + im * im
    power = jnp.sum(mag, axis=1, keepdims=True) / NB
    denom = jnp.sqrt(mag + WATER * power + 1e-06)
    re, im = re / denom, im / denom
    tail = re[:, 384:] + pltpu.roll(im[:, 384:], 64, 1)
    return jnp.concatenate([re[:, :384], im[:, :384], tail], axis=1).astype(jnp.bfloat16)


def kernel(
    n,
    raw_hbm,
    index_ref,
    count_ref,
    tw_ref,
    coarse_ref,
    lagw_ref,
    out_ref,
    x_ref,
    xq_ref,
    base_ref,
    table_ref,
    spec_ref,
    spread_ref,
    lagged_ref,
    load_sem,
    send_sem,
    recv_sem,
    fsend_sem,
    frecv_sem,
):
    slots = raw_hbm.shape[0]
    half = slots // 2
    me = lax.axis_index("chan")
    core = lax.axis_index("pair")
    other = 1 - core

    load = pltpu.make_async_copy(raw_hbm, x_ref, load_sem)
    load.start()

    barrier = pltpu.get_barrier_semaphore()
    pl.semaphore_signal(barrier, inc=1, device_id={"pair": other})
    for d in range(1, n):
        pl.semaphore_signal(barrier, inc=1, device_id={"chan": lax.rem(me + d, n)})

    make_table(tw_ref, coarse_ref, base_ref, table_ref)
    load.wait()
    for q in range(4):
        rows = slice(slots * q, slots * (q + 1))
        xq_ref[rows, 0:QUARTER] = x_ref[:, QUARTER * q : QUARTER * (q + 1)]
        pad = NCHUNK * CHUNK - QUARTER
        xq_ref[rows, QUARTER:] = jnp.zeros((slots, pad), jnp.bfloat16)
    for v in range(2 * PADB // 256):
        cols = slice(256 * v, 256 * v + 256)
        spec_ref[:, cols] = jnp.dot(
            xq_ref[...], table_ref[:, cols], preferred_element_type=jnp.float32
        )
    whitened = whiten_rows(spec_ref, slots)

    r_ids = lax.broadcasted_iota(jnp.int32, (slots, slots), 0)
    k_ids = lax.broadcasted_iota(jnp.int32, (slots, slots), 1)
    chosen = (index_ref[...] == r_ids) & (k_ids < count_ref[me])
    pick = jnp.where(chosen, 1.0, 0.0).T.astype(jnp.bfloat16)
    own = jnp.dot(pick, whitened, preferred_element_type=jnp.float32)
    own16 = own.astype(jnp.bfloat16)
    spread_ref[pl.ds(pl.multiple_of(me * slots, slots), slots), :] = own16

    def part(block, who):
        return spread_ref.at[pl.ds(pl.multiple_of(block * slots + who * half, half), half), :]

    pl.semaphore_wait(barrier, n)

    def direct(d):
        return pltpu.make_async_remote_copy(
            src_ref=part(me, core),
            dst_ref=part(me, core),
            send_sem=send_sem.at[d],
            recv_sem=recv_sem.at[d],
            device_id={"chan": lax.rem(me + d, n)},
        )

    def arrival(d):
        block = lax.rem(me - d + n, n)
        return pltpu.make_async_remote_copy(
            src_ref=part(block, core),
            dst_ref=part(block, core),
            send_sem=send_sem.at[d],
            recv_sem=recv_sem.at[d],
            device_id={"chan": lax.rem(me + d, n)},
        )

    def forward(d, who):
        block = lax.rem(me - d + n, n)
        return pltpu.make_async_remote_copy(
            src_ref=part(block, who),
            dst_ref=part(block, who),
            send_sem=fsend_sem.at[d],
            recv_sem=frecv_sem.at[d],
            device_id={"pair": other},
        )

    for d in range(1, n):
        direct(d).start()
    for l in range(L // 2):
        weight = lagw_ref[core, l : l + 1, :]
        lagged_ref[slots * l : slots * (l + 1), :] = (own * weight).astype(jnp.bfloat16)
    for d in range(1, n):
        arrival(d).wait_recv()
        forward(d, core).start()
    for d in range(1, n):
        forward(d, other).wait_recv()
    for d in range(1, n):
        direct(d).wait_send()
        forward(d, core).wait_send()

    def columns(g, carry):
        at = pl.multiple_of(g * 512, 512)
        product = lax.dot_general(
            lagged_ref[...],
            spread_ref[pl.ds(at, 512), :],
            (((1,), (1,)), ((), ())),
            preferred_element_type=jnp.float32,
        ).astype(jnp.bfloat16)
        for l in range(L // 2):
            out_ref[l, :, pl.ds(at, 512)] = product[slots * l : slots * (l + 1)]
        return carry

    lax.fori_loop(0, n * slots // 512, columns, 0)


def shards(n, raw, live_index, live_count):
    slots = raw.shape[0]
    vmem = pl.BlockSpec(memory_space=pltpu.VMEM)
    return pl.pallas_call(
        functools.partial(kernel, n),
        out_shape=jax.ShapeDtypeStruct((L // 2, slots, n * slots), jnp.bfloat16),
        in_specs=[
            pl.BlockSpec(memory_space=pl.ANY),
            vmem,
            pl.BlockSpec(memory_space=pltpu.SMEM),
            vmem,
            vmem,
            vmem,
        ],
        out_specs=vmem,
        scratch_shapes=[
            pltpu.VMEM((slots, S), jnp.bfloat16),
            pltpu.VMEM((4 * slots, NCHUNK * CHUNK), jnp.bfloat16),
            pltpu.VMEM((CHUNK, 2 * PADB), jnp.float32),
            pltpu.VMEM((NCHUNK * CHUNK, 2 * PADB), jnp.bfloat16),
            pltpu.VMEM((4 * slots, 2 * PADB), jnp.float32),
            pltpu.VMEM((n * slots, COLS), jnp.bfloat16),
            pltpu.VMEM((L // 2 * slots, COLS), jnp.bfloat16),
            pltpu.SemaphoreType.DMA,
            pltpu.SemaphoreType.DMA((n,)),
            pltpu.SemaphoreType.DMA((n,)),
            pltpu.SemaphoreType.DMA((n,)),
            pltpu.SemaphoreType.DMA((n,)),
        ],
        compiler_params=pltpu.CompilerParams(
            collective_id=0, has_side_effects=True, vmem_limit_bytes=60 * 1024 * 1024
        ),
    )(
        raw.reshape(slots, S),
        live_index,
        live_count,
        jnp.asarray(twiddles()),
        jnp.asarray(coarse_twiddles()),
        jnp.asarray(lag_table()),
    )


def solution(mesh):
    return jax.shard_map(
        functools.partial(shards, mesh.shape["chan"]),
        mesh=mesh,
        in_specs=(P(("groups", "chan"), None, None), P(("groups", "chan"), None), P("groups")),
        out_specs=P("pair", ("groups", "chan"), None),
        check_vma=False,
    )
```

time: 119 us -> 22.5 us (0.19)
  other arithmetic: 61.1 us -> 0 us
  blocking collectives: 38.8 us -> 0 us
  Pallas kernels: 0 us -> 20.6 us
  matrix products: 14.2 us -> 0 us
  local copies, waits for them, and re-layouts: 4.09 us -> 1.62 us
    another operation x8 -> x0, other arithmetic: 56.7 us -> none
    all_gather x2 -> x0, blocking collectives: 36.1 us -> none  [the longest x1 34.2 us: shards(): lax.all_gather(own_rows, 'chan', axis=0, tiled=True)]
    pallas_call x0 -> x1, Pallas kernels: none -> 20.6 us  [shards(): pl.pallas_call(functools.partial(kernel, n), out_shape=jax.ShapeDtypeStru...]
    dot_general x9 -> x0, matrix products: 14.2 us -> none  [the longest x8 13.1 us: add_block(): jnp.dot(sample_blk, dft_table, preferred_element_type=jnp.float32)]
    psum x1 -> x0, blocking collectives: 2.63 us -> none  [shards(): lax.psum(jnp.sum(spectrum * spectrum, axis=(2, 3)), 'pair') / NB]
    select_n x2 -> x0, other arithmetic: 2.05 us -> none  [the longest x1 1.39 us: shards(): jnp.where((slot_ids < live_slots)[:, None, None], chosen, jnp.zeros((), r...]
    unnamed x2 -> x1, local copies, waits for them, and re-layouts: 0.01 us -> 1.62 us
    gather x1 -> x0, local copies, waits for them, and re-layouts: 1.53 us -> none  [shards(): chosen = jnp.take(raw, live_index[0], axis=0)]
where the time goes in v1:
time: 22.5 us; the launch traced here: 22.2 us
  Pallas kernels  20.6 us (92%)
  local copies, waits for them, and re-layouts  1.62 us (7%)
    pallas_call x1, Pallas kernels, shards(): pl.pallas_call(functools.partial(kernel, n), out_shape=jax.ShapeDtypeStru...  20.6 us
    unnamed x1, local copies, waits for them, and re-layouts  1.62 us

profile of v1, /device:TPU:0, one launch (start us, length us, event | category | flops | bytes accessed | tf_op | source)
XLA Modules:
  0.0 22.2 jit_solution(3360319599277072685)
XLA Ops:
  0.0 20.6 %shard_map.64 = bf16[3,64,512]{2,1,0:T(8,128)(2,1)} custom-call(bf16[64,12000]{1,0:T(8,128)(2,1)} %bitcast.1, s32[1,64]{1,0:T(1,128)} %index_ref.1, s32[8]{0:T(128)} %count_ref.1, f32[32,1024]{1,0:T(8,128)} %constant.6.clone.tw_ref, f32[12,8,1024]{2,1,0:T(8,128)} %constant.7.clone.coarse_ref, f32[2,8,896]{2,1,0:T(8,128)} %constant.8.clone.lagw_ref), custom_call_target="tpu_custom_call" | custom-call | tf_op jit(solution)/shard_map/pallas_call | solution.py:229
  20.6 1.6 %copy.8 = bf16[3,64,512]{2,1,0:T(8,128)(2,1)} copy(bf16[3,64,512]{2,1,0:T(8,128)(2,1)} %shard_map.64) | data formatting | bytes 393216

commit v2 on v1

--- a/solution.py
+++ b/solution.py
@@ -21,9 +21,9 @@
 COLS = 2 * NB
 
 
-def phase_rows(steps):
+def phase_rows(steps, shift=0.0):
     k = F0 + np.arange(NB)
-    angle = 2.0 * np.pi * ((np.asarray(steps)[:, None] * k[None, :]) % S) / S
+    angle = 2.0 * np.pi * ((np.asarray(steps)[:, None] * k[None, :]) % S) / S + shift
     out = np.zeros((len(steps), 2 * PADB), np.float32)
     out[:, :NB] = np.cos(angle)
     out[:, PADB : PADB + NB] = -np.sin(angle)
@@ -31,7 +31,8 @@
 
 
 def twiddles():
-    fine = phase_rows(np.arange(16))
+    step = 2.0 * np.pi / S
+    fine = phase_rows(np.arange(16), np.pi * (float(np.float32(step)) / step - 1.0))
     mid = phase_rows(16 * np.arange(16))
     return np.concatenate([fine, mid], axis=0)
 
@@ -119,8 +120,10 @@
     spread_ref,
     lagged_ref,
     load_sem,
-    send_sem,
-    recv_sem,
+    zsend_sem,
+    zrecv_sem,
+    xsend_sem,
+    xrecv_sem,
     fsend_sem,
     frecv_sem,
 ):
@@ -133,10 +136,19 @@
     load = pltpu.make_async_copy(raw_hbm, x_ref, load_sem)
     load.start()
 
+    lines = n // 2
+    line, side = me // 2, lax.rem(me, 2)
+    mate = 2 * line + 1 - side
+    order = sorted(range(1, lines), key=lambda d: min(d, lines - d))
+
+    def chip(d, which):
+        return 2 * lax.rem(line + d + lines, lines) + which
+
     barrier = pltpu.get_barrier_semaphore()
     pl.semaphore_signal(barrier, inc=1, device_id={"pair": other})
-    for d in range(1, n):
-        pl.semaphore_signal(barrier, inc=1, device_id={"chan": lax.rem(me + d, n)})
+    pl.semaphore_signal(barrier, inc=1, device_id={"chan": mate})
+    for d in order:
+        pl.semaphore_signal(barrier, inc=1, device_id={"chan": chip(d, side)})
 
     make_table(tw_ref, coarse_ref, base_ref, table_ref)
     load.wait()
@@ -163,64 +175,65 @@
     def part(block, who):
         return spread_ref.at[pl.ds(pl.multiple_of(block * slots + who * half, half), half), :]
 
-    pl.semaphore_wait(barrier, n)
-
-    def direct(d):
+    pl.semaphore_wait(barrier, lines + 1)
+
+    def copy(block, who, sends, recvs, at, device_id):
+        ref = part(block, who)
         return pltpu.make_async_remote_copy(
-            src_ref=part(me, core),
-            dst_ref=part(me, core),
-            send_sem=send_sem.at[d],
-            recv_sem=recv_sem.at[d],
-            device_id={"chan": lax.rem(me + d, n)},
+            src_ref=ref,
+            dst_ref=ref,
+            send_sem=sends.at[at],
+            recv_sem=recvs.at[at],
+            device_id=device_id,
         )
 
-    def arrival(d):
-        block = lax.rem(me - d + n, n)
-        return pltpu.make_async_remote_copy(
-            src_ref=part(block, core),
-            dst_ref=part(block, core),
-            send_sem=send_sem.at[d],
-            recv_sem=recv_sem.at[d],
-            device_id={"chan": lax.rem(me + d, n)},
-        )
-
-    def forward(d, who):
-        block = lax.rem(me - d + n, n)
-        return pltpu.make_async_remote_copy(
-            src_ref=part(block, who),
-            dst_ref=part(block, who),
-            send_sem=fsend_sem.at[d],
-            recv_sem=frecv_sem.at[d],
-            device_id={"pair": other},
-        )
-
-    for d in range(1, n):
-        direct(d).start()
+    def along(d, block):
+        return copy(block, core, zsend_sem, zrecv_sem, d, {"chan": chip(d, side)})
+
+    def across(d, which):
+        return copy(chip(-d, which), core, xsend_sem, xrecv_sem, d, {"chan": mate})
+
+    def inside(d, which, who):
+        at = d + lines * (1 if which is side else 0)
+        return copy(chip(-d, which), who, fsend_sem, frecv_sem, at, {"pair": other})
+
+    far = 1 - side
+    across(0, side).start()
+    for d in order:
+        along(d, me).start()
     for l in range(L // 2):
         weight = lagw_ref[core, l : l + 1, :]
         lagged_ref[slots * l : slots * (l + 1), :] = (own * weight).astype(jnp.bfloat16)
-    for d in range(1, n):
-        arrival(d).wait_recv()
-        forward(d, core).start()
-    for d in range(1, n):
-        forward(d, other).wait_recv()
-    for d in range(1, n):
-        direct(d).wait_send()
-        forward(d, core).wait_send()
-
-    def columns(g, carry):
-        at = pl.multiple_of(g * 512, 512)
+
+    across(0, far).wait_recv()
+    inside(0, far, core).start()
+    for d in order:
+        along(d, chip(-d, side)).wait_recv()
+        across(d, side).start()
+        inside(d, side, core).start()
+
+    for i, d in enumerate([0] + order):
+        if d > 0:
+            across(d, far).wait_recv()
+            inside(d, far, core).start()
+            inside(d, side, other).wait_recv()
+        inside(d, far, other).wait_recv()
+        at = pl.multiple_of(chip(-d, 0) * slots, 2 * slots)
         product = lax.dot_general(
             lagged_ref[...],
-            spread_ref[pl.ds(at, 512), :],
+            spread_ref[pl.ds(at, 2 * slots), :],
             (((1,), (1,)), ((), ())),
             preferred_element_type=jnp.float32,
         ).astype(jnp.bfloat16)
         for l in range(L // 2):
-            out_ref[l, :, pl.ds(at, 512)] = product[slots * l : slots * (l + 1)]
-        return carry
-
-    lax.fori_loop(0, n * slots // 512, columns, 0)
+            out_ref[l, :, pl.ds(at, 2 * slots)] = product[slots * l : slots * (l + 1)]
+
+    for d in [0] + order:
+        across(d, side).wait_send()
+        inside(d, far, core).wait_send()
+        if d > 0:
+            along(d, me).wait_send()
+            inside(d, side, core).wait_send()
 
 
 def shards(n, raw, live_index, live_count):
@@ -228,7 +241,7 @@
     vmem = pl.BlockSpec(memory_space=pltpu.VMEM)
     return pl.pallas_call(
         functools.partial(kernel, n),
-        out_shape=jax.ShapeDtypeStruct((L // 2, slots, n * slots), jnp.bfloat16),
+        out_shape=pltpu.VMEM((L // 2, slots, n * slots), jnp.bfloat16),
         in_specs=[
             pl.BlockSpec(memory_space=pl.ANY),
             vmem,
@@ -247,13 +260,15 @@
             pltpu.VMEM((n * slots, COLS), jnp.bfloat16),
             pltpu.VMEM((L // 2 * slots, COLS), jnp.bfloat16),
             pltpu.SemaphoreType.DMA,
-            pltpu.SemaphoreType.DMA((n,)),
-            pltpu.SemaphoreType.DMA((n,)),
+            pltpu.SemaphoreType.DMA((n // 2,)),
+            pltpu.SemaphoreType.DMA((n // 2,)),
+            pltpu.SemaphoreType.DMA((n // 2,)),
+            pltpu.SemaphoreType.DMA((n // 2,)),
             pltpu.SemaphoreType.DMA((n,)),
             pltpu.SemaphoreType.DMA((n,)),
         ],
         compiler_params=pltpu.CompilerParams(
-            collective_id=0, has_side_effects=True, vmem_limit_bytes=60 * 1024 * 1024
+            collective_id=0, has_side_effects=True, vmem_limit_bytes=44 * 1024 * 1024
         ),
     )(
         raw.reshape(slots, S),

time: 22.5 us -> 26.9 us (1.20)
  local copies, waits for them, and re-layouts: 1.62 us -> 6.1 us
  Pallas kernels: 20.6 us -> 20.3 us
    unnamed x1 -> x13, local copies, waits for them, and re-layouts: 1.62 us -> 6.1 us
where the time goes in v2:
time: 26.9 us; the launch traced here: 26.4 us
  Pallas kernels  20.3 us (75%)
  local copies, waits for them, and re-layouts  6.1 us (23%)
    pallas_call x1, Pallas kernels, shards(): pl.pallas_call(functools.partial(kernel, n), out_shape=pltpu.VMEM((L // 2...  20.3 us
    unnamed x13, local copies, waits for them, and re-layouts  6.1 us

profile of v2, /device:TPU:0, one launch (start us, length us, event | category | flops | bytes accessed | tf_op | source)
XLA Modules:
  0.0 26.4 jit_solution(9188761395559101028)
XLA Ops:
  0.0 0.0 copy-start
  0.0 1.4 %copy-done = bf16[64,1,12000]{2,0,1:T(8,128)(2,1)S(1)} copy-done((bf16[64,1,12000]{2,0,1:T(8,128)(2,1)S(1)}, bf16[64,1,12000]{2,0,1:T(8,128)(2,1)}, u32[]{:S(2)}) %copy-start) | copy-done | bytes 1536024
  1.4 0.0 copy-start.1
  1.4 1.0 %copy-done.1 = f32[12,8,1024]{2,1,0:T(8,128)S(1)} copy-done((f32[12,8,1024]{2,1,0:T(8,128)S(1)}, f32[12,8,1024]{2,1,0:T(8,128)}, u32[]{:S(2)}) %copy-start.1) | copy-done | bytes 393240
  2.4 0.0 copy-start.2
  2.4 0.9 %copy-done.2 = f32[32,1024]{1,0:T(8,128)S(1)} copy-done((f32[32,1024]{1,0:T(8,128)S(1)}, f32[32,1024]{1,0:T(8,128)}, u32[]{:S(2)}) %copy-start.2) | copy-done | bytes 131096
  3.3 0.0 copy-start.3
  3.3 0.8 %copy-done.3 = f32[2,8,896]{2,1,0:T(8,128)S(1)} copy-done((f32[2,8,896]{2,1,0:T(8,128)S(1)}, f32[2,8,896]{2,1,0:T(8,128)}, u32[]{:S(2)}) %copy-start.3) | copy-done | bytes 57368
  4.1 0.0 copy-start.4
  4.1 0.7 %copy-done.4 = s32[1,64]{1,0:T(1,128)S(1)} copy-done((s32[1,64]{1,0:T(1,128)S(1)}, s32[1,64]{1,0:T(1,128)}, u32[]{:S(2)}) %copy-start.4) | copy-done | bytes 280
  4.8 0.0 copy-start.5
  4.8 0.7 %copy-done.5 = s32[8]{0:T(128)S(1)} copy-done((s32[8]{0:T(128)S(1)}, s32[8]{0:T(128)}, u32[]{:S(2)}) %copy-start.5) | copy-done | bytes 56
  5.4 20.3 %shard_map.64 = bf16[3,64,512]{2,1,0:T(8,128)(2,1)S(1)} custom-call(bf16[64,12000]{1,0:T(8,128)(2,1)S(1)} %bitcast.1, s32[1,64]{1,0:T(1,128)S(1)} %copy-done.4, s32[8]{0:T(128)S(1)} %copy-done.5, f32[32,1024]{1,0:T(8,128)S(1)} %copy-done.2, f32[12,8,1024]{2,1,0:T(8,128)S(1)} %copy-done.1, f32[2,8,896]{2,1,0:T(8,128)S(1)} %copy-done.3), custom_call_target="tpu_custom_call" | custom-call | tf_op jit(solution)/shard_map/pallas_call | solution.py:242
  25.7 0.7 %copy.8 = bf16[3,64,512]{2,1,0:T(8,128)(2,1)} copy(bf16[3,64,512]{2,1,0:T(8,128)(2,1)S(1)} %shard_map.64) | data formatting | bytes 393216
Async XLA Ops:
  0.0 1.4 %copy-start = (bf16[64,1,12000]{2,0,1:T(8,128)(2,1)S(1)}, bf16[64,1,12000]{2,0,1:T(8,128)(2,1)}, u32[]{:S(2)}) copy-start(bf16[64,1,12000]{2,0,1:T(8,128)(2,1)} %param.6) | copy-start | bytes 4608004
  1.4 1.0 %copy-start.1 = (f32[12,8,1024]{2,1,0:T(8,128)S(1)}, f32[12,8,1024]{2,1,0:T(8,128)}, u32[]{:S(2)}) copy-start(f32[12,8,1024]{2,1,0:T(8,128)} %constant.7.clone.coarse_ref) | copy-start | bytes 1179652
  2.4 0.9 %copy-start.2 = (f32[32,1024]{1,0:T(8,128)S(1)}, f32[32,1024]{1,0:T(8,128)}, u32[]{:S(2)}) copy-start(f32[32,1024]{1,0:T(8,128)} %constant.6.clone.tw_ref) | copy-start | bytes 393220
  3.3 0.8 %copy-start.3 = (f32[2,8,896]{2,1,0:T(8,128)S(1)}, f32[2,8,896]{2,1,0:T(8,128)}, u32[]{:S(2)}) copy-start(f32[2,8,896]{2,1,0:T(8,128)} %constant.8.clone.lagw_ref) | copy-start | bytes 172036
  4.1 0.7 %copy-start.4 = (s32[1,64]{1,0:T(1,128)S(1)}, s32[1,64]{1,0:T(1,128)}, u32[]{:S(2)}) copy-start(s32[1,64]{1,0:T(1,128)} %index_ref.1) | copy-start | bytes 772
  4.8 0.7 %copy-start.5 = (s32[8]{0:T(128)S(1)}, s32[8]{0:T(128)}, u32[]{:S(2)}) copy-start(s32[8]{0:T(128)} %count_ref.1) | copy-start | bytes 100

commit v3 on v2

--- a/solution.py
+++ b/solution.py
@@ -19,6 +19,7 @@
 NCHUNK = -(-QUARTER // CHUNK)
 PADB = 512
 COLS = 2 * NB
+VMEM_LIMIT = 63_300_000
 
 
 def phase_rows(steps, shift=0.0):
@@ -30,16 +31,12 @@
     return out
 
 
-def twiddles():
+def constants():
     step = 2.0 * np.pi / S
     fine = phase_rows(np.arange(16), np.pi * (float(np.float32(step)) / step - 1.0))
     mid = phase_rows(16 * np.arange(16))
-    return np.concatenate([fine, mid], axis=0)
-
-
-def coarse_twiddles():
-    coarse = phase_rows(CHUNK * np.arange(NCHUNK))
-    return np.repeat(coarse[:, None, :], 8, axis=1)
+    coarse = np.repeat(phase_rows(CHUNK * np.arange(NCHUNK)), 8, axis=0)
+    return np.concatenate([fine, mid, coarse, lag_table()], axis=0)
 
 
 def column_bins():
@@ -52,12 +49,12 @@
     taper = 0.5 - 0.5 * np.cos(2.0 * np.pi * (j + 0.5) / NB)
     lags = np.arange(L)[:, None] * LSTEP
     waves = np.cos(2.0 * np.pi * (((F0 + j)[None, :] * lags) % S) / S)
-    table = np.zeros((2, 8, COLS), np.float32)
-    table[:, : L // 2] = (taper[None, :] * waves / np.sqrt(NB)).reshape(2, L // 2, COLS)
-    return table
-
-
-def make_table(tw_ref, coarse_ref, base_ref, table_ref):
+    table = np.zeros((2, 8, 2 * PADB), np.float32)
+    table[:, : L // 2, :COLS] = (taper[None, :] * waves / np.sqrt(NB)).reshape(2, L // 2, COLS)
+    return table.reshape(16, 2 * PADB)
+
+
+def make_table(tw_ref, base_ref, table_ref):
     for a in range(16):
         for v in range(PADB // 128):
             c_cols = slice(128 * v, 128 * v + 128)
@@ -72,8 +69,9 @@
         for v in range(PADB // 128):
             c_cols = slice(128 * v, 128 * v + 128)
             s_cols = slice(PADB + 128 * v, PADB + 128 * v + 128)
-            cc = coarse_ref[i, 0:1, c_cols]
-            cs = coarse_ref[i, 0:1, s_cols]
+            at = pl.ds(pl.multiple_of(32 + 8 * i, 8), 8)
+            cc = jnp.concatenate([tw_ref[at, c_cols]] * 2, axis=0)
+            cs = jnp.concatenate([tw_ref[at, s_cols]] * 2, axis=0)
             for r in range(0, CHUNK, 16):
                 bc, bs = base_ref[r : r + 16, c_cols], base_ref[r : r + 16, s_cols]
                 rows = pl.ds(row0 + r, 16)
@@ -108,10 +106,9 @@
     raw_hbm,
     index_ref,
     count_ref,
+    tw_hbm,
+    out_ref,
     tw_ref,
-    coarse_ref,
-    lagw_ref,
-    out_ref,
     x_ref,
     xq_ref,
     base_ref,
@@ -120,6 +117,7 @@
     spread_ref,
     lagged_ref,
     load_sem,
+    tw_sem,
     zsend_sem,
     zrecv_sem,
     xsend_sem,
@@ -134,15 +132,21 @@
     other = 1 - core
 
     load = pltpu.make_async_copy(raw_hbm, x_ref, load_sem)
+    tw_load = pltpu.make_async_copy(tw_hbm, tw_ref, tw_sem)
+    tw_load.start()
     load.start()
 
     lines = n // 2
     line, side = me // 2, lax.rem(me, 2)
     mate = 2 * line + 1 - side
-    order = sorted(range(1, lines), key=lambda d: min(d, lines - d))
+    order = list(range(1, lines))
 
     def chip(d, which):
-        return 2 * lax.rem(line + d + lines, lines) + which
+        row = line
+        for bit in range(lines.bit_length()):
+            if d >> bit & 1:
+                row = row + (1 << bit) - (2 << bit) * (line // (1 << bit) % 2)
+        return 2 * row + which
 
     barrier = pltpu.get_barrier_semaphore()
     pl.semaphore_signal(barrier, inc=1, device_id={"pair": other})
@@ -150,7 +154,8 @@
     for d in order:
         pl.semaphore_signal(barrier, inc=1, device_id={"chan": chip(d, side)})
 
-    make_table(tw_ref, coarse_ref, base_ref, table_ref)
+    tw_load.wait()
+    make_table(tw_ref, base_ref, table_ref)
     load.wait()
     for q in range(4):
         rows = slice(slots * q, slots * (q + 1))
@@ -191,24 +196,26 @@
         return copy(block, core, zsend_sem, zrecv_sem, d, {"chan": chip(d, side)})
 
     def across(d, which):
-        return copy(chip(-d, which), core, xsend_sem, xrecv_sem, d, {"chan": mate})
+        return copy(chip(d, which), core, xsend_sem, xrecv_sem, d, {"chan": mate})
 
     def inside(d, which, who):
         at = d + lines * (1 if which is side else 0)
-        return copy(chip(-d, which), who, fsend_sem, frecv_sem, at, {"pair": other})
+        return copy(chip(d, which), who, fsend_sem, frecv_sem, at, {"pair": other})
 
     far = 1 - side
     across(0, side).start()
     for d in order:
         along(d, me).start()
+    lag_at = pl.multiple_of(32 + 8 * NCHUNK + 8 * core, 8)
+    weights = tw_ref[pl.ds(lag_at, 8), :COLS]
     for l in range(L // 2):
-        weight = lagw_ref[core, l : l + 1, :]
+        weight = weights[l : l + 1, :]
         lagged_ref[slots * l : slots * (l + 1), :] = (own * weight).astype(jnp.bfloat16)
 
     across(0, far).wait_recv()
     inside(0, far, core).start()
     for d in order:
-        along(d, chip(-d, side)).wait_recv()
+        along(d, chip(d, side)).wait_recv()
         across(d, side).start()
         inside(d, side, core).start()
 
@@ -218,7 +225,7 @@
             inside(d, far, core).start()
             inside(d, side, other).wait_recv()
         inside(d, far, other).wait_recv()
-        at = pl.multiple_of(chip(-d, 0) * slots, 2 * slots)
+        at = pl.multiple_of(chip(d, 0) * slots, 2 * slots)
         product = lax.dot_general(
             lagged_ref[...],
             spread_ref[pl.ds(at, 2 * slots), :],
@@ -246,12 +253,11 @@
             pl.BlockSpec(memory_space=pl.ANY),
             vmem,
             pl.BlockSpec(memory_space=pltpu.SMEM),
-            vmem,
-            vmem,
-            vmem,
+            pl.BlockSpec(memory_space=pl.ANY),
         ],
         out_specs=vmem,
         scratch_shapes=[
+            pltpu.VMEM((48 + 8 * NCHUNK, 2 * PADB), jnp.float32),
             pltpu.VMEM((slots, S), jnp.bfloat16),
             pltpu.VMEM((4 * slots, NCHUNK * CHUNK), jnp.bfloat16),
             pltpu.VMEM((CHUNK, 2 * PADB), jnp.float32),
@@ -260,6 +266,7 @@
             pltpu.VMEM((n * slots, COLS), jnp.bfloat16),
             pltpu.VMEM((L // 2 * slots, COLS), jnp.bfloat16),
             pltpu.SemaphoreType.DMA,
+            pltpu.SemaphoreType.DMA,
             pltpu.SemaphoreType.DMA((n // 2,)),
             pltpu.SemaphoreType.DMA((n // 2,)),
             pltpu.SemaphoreType.DMA((n // 2,)),
@@ -268,15 +275,13 @@
             pltpu.SemaphoreType.DMA((n,)),
         ],
         compiler_params=pltpu.CompilerParams(
-            collective_id=0, has_side_effects=True, vmem_limit_bytes=44 * 1024 * 1024
+            collective_id=0, has_side_effects=True, vmem_limit_bytes=VMEM_LIMIT - 6 * slots * n * slots
         ),
     )(
         raw.reshape(slots, S),
         live_index,
         live_count,
-        jnp.asarray(twiddles()),
-        jnp.asarray(coarse_twiddles()),
-        jnp.asarray(lag_table()),
+        jnp.asarray(constants()),
     )
 
 

time: 26.9 us -> 21.2 us (0.79)
  local copies, waits for them, and re-layouts: 6.1 us -> 0.68 us
    unnamed x13 -> x1, local copies, waits for them, and re-layouts: 6.1 us -> 0.68 us
where the time goes in v3:
time: 21.2 us; the launch traced here: 20.9 us
  Pallas kernels  20.2 us (95%)
  local copies, waits for them, and re-layouts  0.68 us (3%)
    pallas_call x1, Pallas kernels, shards(): pl.pallas_call(functools.partial(kernel, n), out_shape=pltpu.VMEM((L // 2...  20.2 us
    unnamed x1, local copies, waits for them, and re-layouts  0.68 us

profile of v3, /device:TPU:0, one launch (start us, length us, event | category | flops | bytes accessed | tf_op | source)
XLA Modules:
  0.0 20.9 jit_solution(9100824445138873940)
XLA Ops:
  0.0 20.2 %shard_map.46 = bf16[3,64,512]{2,1,0:T(8,128)(2,1)S(1)} custom-call(bf16[64,12000]{1,0:T(8,128)(2,1)} %bitcast.1, s32[1,64]{1,0:T(1,128)} %index_ref.1, s32[8]{0:T(128)} %count_ref.1, f32[144,1024]{1,0:T(8,128)} %constant.2.clone.tw_hbm), custom_call_target="tpu_custom_call" | custom-call | tf_op jit(solution)/shard_map/pallas_call | solution.py:249
  20.2 0.7 %copy.6 = bf16[3,64,512]{2,1,0:T(8,128)(2,1)} copy(bf16[3,64,512]{2,1,0:T(8,128)(2,1)S(1)} %shard_map.46) | data formatting | bytes 393216

commit v4 on v3

--- a/solution.py
+++ b/solution.py
@@ -204,7 +204,7 @@
 
     far = 1 - side
     across(0, side).start()
-    for d in order:
+    for d in reversed(order):
         along(d, me).start()
     lag_at = pl.multiple_of(32 + 8 * NCHUNK + 8 * core, 8)
     weights = tw_ref[pl.ds(lag_at, 8), :COLS]

time: 21.2 us -> 23 us (1.085)
  Pallas kernels: 20.2 us -> 22.1 us
    pallas_call x1, Pallas kernels: 20.2 us -> 22.1 us  [shards(): pl.pallas_call(functools.partial(kernel, n), out_shape=pltpu.VMEM((L // 2...]
where the time goes in v4:
time: 23 us; the launch traced here: 22.8 us
  Pallas kernels  22.1 us (96%)
  local copies, waits for them, and re-layouts  0.68 us (3%)
    pallas_call x1, Pallas kernels, shards(): pl.pallas_call(functools.partial(kernel, n), out_shape=pltpu.VMEM((L // 2...  22.1 us
    unnamed x1, local copies, waits for them, and re-layouts  0.68 us

profile of v4, /device:TPU:0, one launch (start us, length us, event | category | flops | bytes accessed | tf_op | source)
XLA Modules:
  0.0 22.8 jit_solution(14674599627505354304)
XLA Ops:
  0.0 22.1 %shard_map.46 = bf16[3,64,512]{2,1,0:T(8,128)(2,1)S(1)} custom-call(bf16[64,12000]{1,0:T(8,128)(2,1)} %bitcast.1, s32[1,64]{1,0:T(1,128)} %index_ref.1, s32[8]{0:T(128)} %count_ref.1, f32[144,1024]{1,0:T(8,128)} %constant.2.clone.tw_hbm), custom_call_target="tpu_custom_call" | custom-call | tf_op jit(solution)/shard_map/pallas_call | solution.py:249
  22.1 0.7 %copy.6 = bf16[3,64,512]{2,1,0:T(8,128)(2,1)} copy(bf16[3,64,512]{2,1,0:T(8,128)(2,1)S(1)} %shard_map.46) | data formatting | bytes 393216
